TPU v7x, 128 devices: a whole 4x4x4 slice. The times are simulated.
128 devices in a mesh: row: 4 (over y), col: 32 (over z, x, core).
Axes of the slice: x: 4, y: 4, z: 4, core: 2. Of those that a mesh axis runs over, the one named last changes fastest.
Arguments:
- tokens: bfloat16 [768, 8192], P('col', 'row'), may hold values from -6 to 6
- gate_weight: bfloat16 [8192, 28672], P('row', 'col'), may hold values from -0.0625 to 0.0625
- up_weight: bfloat16 [8192, 28672], P('row', 'col'), may hold values from -0.0625 to 0.0625
- down_weight: bfloat16 [28672, 8192], P('col', 'row'), may hold values from -0.03125 to 0.03125
- mask_gate: int32 [128, 448], P('row', 'col'), may hold values from 0 to 1, as said below
- mask_up: int32 [128, 448], P('row', 'col'), may hold values from 0 to 1, as said below
- mask_down: int32 [448, 128], P('col', 'row'), may hold values from 0 to 1, as said below
- cotangent: bfloat16 [768, 8192], P('col', 'row'), may hold values from -1.5 to 1.5
Outputs:
- output: bfloat16 [768, 8192], P('col', 'row')
- grad_input: bfloat16 [768, 8192], P('col', 'row')
- grad_gate: bfloat16 [8192, 28672], P('row', 'col')
- grad_up: bfloat16 [8192, 28672], P('row', 'col')
- grad_down: bfloat16 [28672, 8192], P('col', 'row')
Inputs may be any that keep to these rules, and one draw needn't show every extreme that they name: `mask_gate`: 1 where a 64 x 64 block of the weight is kept, 0 where it is pruned. `mask_up`: 1 where a 64 x 64 block of the weight is kept, 0 where it is pruned. `mask_down`: 1 where a 64 x 64 block of the weight is kept, 0 where it is pruned.
All inputs are finite; a program needn't handle non-finite values.
Results may differ from a plain program's by a relative error of at most 0.006.
Values may be sent and summed in bfloat16 or wider, within the bound.
No kernel may reach another device: no remote copies, remote signals or barrier semaphores. Data moves between devices by JAX's collectives and lax.ppermute only.
A program may use at most 128 MiB of HBM per device.

v0:
```python
import jax
import jax.numpy as jnp
from jax import lax
from jax.sharding import PartitionSpec as P

BLOCK = 64


def expand(mask):
    return jnp.repeat(jnp.repeat(mask, BLOCK, 0), BLOCK, 1).astype(jnp.bfloat16)


def contract_last(left, right):
    return lax.dot_general(
        left, right, (((1,), (1,)), ((), ())), preferred_element_type=jnp.float32
    )


def contract_first(left, right):
    return lax.dot_general(
        left, right, (((0,), (0,)), ((), ())), preferred_element_type=jnp.float32
    )


def backward_gates(dhid, gate, up):
    sigma = jax.nn.sigmoid(gate)
    dgate = (dhid * up * sigma * (1.0 + gate * (1.0 - sigma))).astype(jnp.bfloat16)
    dup = (dhid * gate * sigma).astype(jnp.bfloat16)
    return (dgate, dup)


def body(tokens, gate_weight, up_weight, down_weight, mask_gate, mask_up, mask_down, cotangent):
    keep_gate = expand(mask_gate)
    keep_up = expand(mask_up)
    keep_down = expand(mask_down)
    w_gate = gate_weight * keep_gate
    w_up = up_weight * keep_up
    w_down = down_weight * keep_down
    width = w_gate.shape[1]
    pair = lax.all_gather(jnp.concatenate([tokens, cotangent], axis=1), "col", axis=0, tiled=True)
    depth = tokens.shape[1]
    panel = pair[:, :depth]
    cot_panel = pair[:, depth:]
    parts = jnp.concatenate(
        [
            jnp.dot(panel, w_gate, preferred_element_type=jnp.float32).astype(jnp.bfloat16),
            jnp.dot(panel, w_up, preferred_element_type=jnp.float32).astype(jnp.bfloat16),
            contract_last(cot_panel, w_down).astype(jnp.bfloat16),
        ],
        axis=1,
    )
    rows = parts.shape[0] // 4
    swapped = lax.all_to_all(parts, "row", 0, 0, tiled=True)
    total = jnp.sum(swapped.reshape(4, rows, 3 * width).astype(jnp.float32), axis=0)
    gate = total[:, :width]
    up = total[:, width : 2 * width]
    dhid = total[:, 2 * width :]
    hidden = (jax.nn.silu(gate) * up).astype(jnp.bfloat16)
    dgate, dup = backward_gates(dhid, gate, up)
    whole = lax.all_gather(jnp.concatenate([hidden, dgate, dup], axis=1), "row", axis=0, tiled=True)
    hidden = whole[:, :width]
    dgate = whole[:, width : 2 * width]
    dup = whole[:, 2 * width :]
    both = jnp.concatenate(
        [
            jnp.dot(hidden, w_down, preferred_element_type=jnp.float32).astype(jnp.bfloat16),
            (contract_last(dgate, w_gate) + contract_last(dup, w_up)).astype(jnp.bfloat16),
        ],
        axis=1,
    )
    spread = lax.all_to_all(both, "col", 0, 0, tiled=True)
    grad_down = (contract_first(hidden, cot_panel) * keep_down).astype(jnp.bfloat16)
    grad_gate = (contract_first(panel, dgate) * keep_gate).astype(jnp.bfloat16)
    grad_up = (contract_first(panel, dup) * keep_up).astype(jnp.bfloat16)
    spread = spread.reshape(-1, tokens.shape[0], 2 * depth).astype(jnp.float32)
    owned = jnp.sum(spread, axis=0).astype(jnp.bfloat16)
    output = owned[:, :depth]
    grad_input = owned[:, depth:]
    return (output, grad_input, grad_gate, grad_up, grad_down)


def solution(mesh):
    return jax.shard_map(
        body,
        mesh=mesh,
        in_specs=(
            P("col", "row"),
            P("row", "col"),
            P("row", "col"),
            P("col", "row"),
            P("row", "col"),
            P("row", "col"),
            P("col", "row"),
            P("col", "row"),
        ),
        out_specs=(
            P("col", "row"),
            P("col", "row"),
            P("row", "col"),
            P("row", "col"),
            P("col", "row"),
        ),
        check_vma=False,
    )
```

profile of v0, /device:TPU:0, one launch (start us, length us, event | category | flops | bytes accessed | tf_op | source)
XLA Modules:
  0.0 288.6 jit_solution(12454030804781257054)
XLA Ops:
  7.2 0.0 all-gather.3.cloned.1.call-start
  7.2 1.6 pad_maximum_fusion.3
  8.8 0.0 all-gather.3.cloned.1.call-update
  8.9 0.0 all-gather.5.cloned.1.call-start
  8.9 0.7 convert_element_type.88
  9.6 0.1 copy.24
  9.7 0.1 broadcast_in_dim.22
  9.9 0.1 convert_element_type.89
  10.0 0.0 copy-start.8
  10.0 6.1 %copy.25 = bf16[896,2048]{0,1:T(8,128)(2,1)} copy(bf16[896,2048]{1,0:T(8,128)(2,1)} %param.11) | data formatting | bytes 7340032 | tf_op args[3]
  16.1 0.1 broadcast_in_dim.20
  16.2 0.2 convert_element_type.85
  16.4 6.1 %copy.23 = bf16[2048,896]{0,1:T(8,128)(2,1)} copy(bf16[2048,896]{1,0:T(8,128)(2,1)} %param.10) | data formatting | bytes 7340032 | tf_op args[2]
  22.4 0.1 broadcast_in_dim.18
  22.6 0.1 convert_element_type.81
  22.7 6.1 %copy.22 = bf16[2048,896]{0,1:T(8,128)(2,1)} copy(bf16[2048,896]{1,0:T(8,128)(2,1)} %param.9) | data formatting | bytes 7340032 | tf_op args[1]
  28.8 4.4 %bitcast_multiply_fusion = bf16[896,2048]{0,1:T(8,128)(2,1)} fusion(bf16[896,2048]{0,1:T(8,128)(2,1)} %copy.25, bf16[896,32]{0,1:T(8,128)(2,1)S(1)} %convert_element_type.89), kind=kLoop, calls=%fused_computation.17 | loop fusion | flops 1835008 | bytes 7397376 | tf_op jit(solution)/shard_map/mul | solution.py:38
  33.2 2.1 bitcast_multiply_fusion.1
  35.3 1.2 copy-done.1
  36.6 2.1 bitcast_multiply_fusion.2
  38.7 23.2 %all-gather.3.cloned.1.call-done = bf16[768,4096]{1,0:T(8,128)(2,1)} async-done(((bf16[24,4096]{1,0:T(8,128)(2,1)}), bf16[768,4096]{1,0:T(8,128)(2,1)}) %all-gather.3.cloned.1.call-update) | async-done | bytes 6291472 | tf_op jit(solution)/shard_map/all_gather | solution.py:40
  61.9 6.5 %fusion.15 = bf16[768,896]{1,0:T(8,128)(2,1)S(1)} fusion(bf16[896,2048]{0,1:T(8,128)(2,1)} %bitcast_multiply_fusion, bf16[768,4096]{1,0:T(8,128)(2,1)} %all-gather.3.cloned.1.call-done), kind=kOutput, calls=%fused_computation.22 | convolution fusion | flops 2819260416 | bytes 8192000 | tf_op jit(solution)/shard_map/dot_general | solution.py:14
  68.4 3.5 %fusion.12 = bf16[768,896]{1,0:T(8,128)(2,1)S(1)} fusion(bf16[2048,896]{0,1:T(8,128)(2,1)S(1)} %copy-done.2, bf16[768,4096]{1,0:T(8,128)(2,1)S(1)} %copy-done.10), kind=kOutput, calls=%fused_computation.21 | convolution fusion | flops 2819260416 | bytes 8192000 | tf_op jit(solution)/shard_map/dot_general | solution.py:47
  71.9 3.4 %fusion.9 = bf16[768,896]{1,0:T(8,128)(2,1)S(1)} fusion(bf16[2048,896]{0,1:T(8,128)(2,1)S(1)} %copy-done.4, bf16[768,4096]{1,0:T(8,128)(2,1)S(1)} %copy-done.10), kind=kOutput, calls=%fused_computation.20 | convolution fusion | flops 2819260416 | bytes 8192000 | tf_op jit(solution)/shard_map/dot_general | solution.py:46
  75.4 0.4 pad_maximum_fusion.1
  75.7 52.6 %all_to_all.18 = bf16[4,192,2688]{2,1,0:T(8,128)(2,1)S(1)} all-to-all(bf16[4,192,2688]{2,1,0:T(8,128)(2,1)S(1)} %bitcast.21), channel_id=1, replica_groups=mesh['row'=4,'col'=32] {'row'}, dimensions={0} | all-to-all | bytes 8257536 | tf_op jit(solution)/shard_map/all_to_all | solution.py:53
  128.3 0.6 convert_reduce_fusion
  128.9 0.4 multiply_convert_fusion.5
  129.3 1.0 pad_maximum_fusion.2
  130.4 0.0 all-gather.5.cloned.1.call-update
  130.4 44.7 %all-gather.5.cloned.1.call-done = bf16[768,2688]{1,0:T(8,128)(2,1)} async-done(((bf16[192,2688]{1,0:T(8,128)(2,1)}), bf16[768,2688]{1,0:T(8,128)(2,1)}) %all-gather.5.cloned.1.call-update) | async-done | bytes 4128784 | tf_op jit(solution)/shard_map/all_gather | solution.py:60
  175.1 6.0 %convolution_convert_fusion = bf16[768,2048]{1,0:T(8,128)(2,1)S(1)} fusion(bf16[896,2048]{0,1:T(8,128)(2,1)} %bitcast_multiply_fusion, bf16[768,2688]{1,0:T(8,128)(2,1)} %all-gather.5.cloned.1.call-done), kind=kOutput, calls=%fused_computation.7 | convolution fusion | flops 2820145152 | bytes 8192000 | tf_op jit(solution)/shard_map/dot_general | solution.py:66
  181.2 3.4 %fusion.21 = f32[768,2048]{1,0:T(8,128)S(1)} fusion(bf16[2048,896]{0,1:T(8,128)(2,1)S(1)} %copy-done.5, bf16[768,2688]{1,0:T(8,128)(2,1)S(1)} %copy-done.11), kind=kOutput, calls=%fused_computation.26 | convolution fusion | flops 2818572288 | bytes 11337728 | tf_op jit(solution)/shard_map/dot_general | solution.py:14
  184.6 3.7 %add_convert_fusion = bf16[768,2048]{1,0:T(8,128)(2,1)S(1)} fusion(f32[768,2048]{1,0:T(8,128)S(1)} %fusion.21, bf16[2048,896]{0,1:T(8,128)(2,1)S(1)} %copy-done.3, bf16[768,2688]{1,0:T(8,128)(2,1)S(1)} %copy-done.11), kind=kOutput, calls=%fused_computation.5 | convolution fusion | flops 2821718016 | bytes 14483456 | tf_op jit(solution)/shard_map/dot_general | solution.py:14
  188.4 3.4 %pad_maximum_fusion = bf16[768,4096]{1,0:T(8,128)(2,1)} fusion(bf16[768,2048]{1,0:T(8,128)(2,1)S(1)} %add_convert_fusion, bf16[768,2048]{1,0:T(8,128)(2,1)S(1)} %convolution_convert_fusion), kind=kLoop, calls=%fused_computation.4 | loop fusion | flops 12582912 | bytes 12582912 | tf_op jit(solution)/shard_map/concatenate | solution.py:64
  191.8 7.6 %all-to-all-start.1 = ((bf16[32,24,4096]{2,1,0:T(8,128)(2,1)}), bf16[32,24,4096]{2,1,0:T(8,128)(2,1)}, u32[]{:S(2)}, u32[]{:S(2)}) async-start(bf16[32,24,4096]{2,1,0:T(8,128)(2,1)} %bitcast.20), calls=%async_computation.1 | async-start | bytes 12582912 | tf_op jit(solution)/shard_map/all_to_all | solution.py:71
  199.3 2.1 broadcast_in_dim.23
  201.5 6.1 %copy.28 = bf16[896,2048]{1,0:T(8,128)(2,1)} copy(bf16[896,2048]{0,1:T(8,128)(2,1)} %bitcast.22) | data formatting | bytes 7340032 | tf_op jit(solution)/shard_map/convert_element_type | solution.py:10
  207.6 2.3 broadcast_in_dim.21
  209.9 6.0 %copy.27 = bf16[2048,896]{1,0:T(8,128)(2,1)} copy(bf16[2048,896]{0,1:T(8,128)(2,1)} %bitcast.23) | data formatting | bytes 7340032 | tf_op jit(solution)/shard_map/convert_element_type | solution.py:10
  215.9 2.3 broadcast_in_dim.19
  218.2 6.2 %copy.26 = bf16[2048,896]{1,0:T(8,128)(2,1)} copy(bf16[2048,896]{0,1:T(8,128)(2,1)} %bitcast.24) | data formatting | bytes 7340032 | tf_op jit(solution)/shard_map/convert_element_type | solution.py:10
  224.4 8.5 %multiply_convert_fusion = bf16[896,2048]{1,0:T(8,128)(2,1)} fusion(bf16[896,2048]{1,0:T(8,128)(2,1)} %copy.28, bf16[768,4096]{1,0:T(8,128)(2,1)} %all-gather.3.cloned.1.call-done, bf16[768,2688]{1,0:T(8,128)(2,1)} %all-gather.5.cloned.1.call-done), kind=kOutput, calls=%fused_computation.1 | convolution fusion | flops 2824077312 | bytes 11862016 | tf_op jit(solution)/shard_map/dot_general | solution.py:20
  232.9 5.1 %multiply_convert_fusion.1 = bf16[2048,896]{1,0:T(8,128)(2,1)} fusion(bf16[2048,896]{1,0:T(8,128)(2,1)S(1)} %copy-done.6, bf16[768,4096]{1,0:T(8,128)(2,1)S(1)} %bitcast.26, bf16[768,2688]{1,0:T(8,128)(2,1)S(1)} %copy-done.12), kind=kOutput, calls=%fused_computation.2 | convolution fusion | flops 2824077312 | bytes 11862016 | tf_op jit(solution)/shard_map/dot_general | solution.py:20
  238.0 5.1 %multiply_convert_fusion.2 = bf16[2048,896]{1,0:T(8,128)(2,1)} fusion(bf16[2048,896]{1,0:T(8,128)(2,1)S(1)} %copy-done.7, bf16[768,4096]{1,0:T(8,128)(2,1)S(1)} %bitcast.26, bf16[768,2688]{1,0:T(8,128)(2,1)S(1)} %copy-done.12), kind=kOutput, calls=%fused_computation.3 | convolution fusion | flops 2824077312 | bytes 11862016 | tf_op jit(solution)/shard_map/dot_general | solution.py:20
  243.1 33.9 %all-to-all-done.1 = bf16[32,24,4096]{2,1,0:T(8,128)(2,1)} async-done(((bf16[32,24,4096]{2,1,0:T(8,128)(2,1)}), bf16[32,24,4096]{2,1,0:T(8,128)(2,1)}, u32[]{:S(2)}, u32[]{:S(2)}) %all-to-all-start.1) | async-done | bytes 6291488 | tf_op jit(solution)/shard_map/all_to_all | solution.py:71
  277.0 4.1 %reduce_sum.22 = bf16[24,4096]{1,0:T(8,128)(2,1)S(1)} reduce(bf16[32,24,4096]{2,1,0:T(8,128)(2,1)} %all-to-all-done.1, bf16[]{:T(256)} %constant.7.clone.1), dimensions={0}, to_apply=%region_1.2 | reduce | flops 3047424 | bytes 6488066 | tf_op jit(solution)/shard_map/reduce_sum | solution.py:76
  281.1 0.7 fusion.25
  (31 shorter events, 0.1 us)
Async XLA Ops:
  7.2 54.7 %all-gather.3.cloned.1.call-start = ((), (), s32[]{:S(2)}) async-start(), calls=%async_computation.2 | async-start | bytes 6488064 | tf_op jit(solution)/shard_map/all_gather | solution.py:40
  8.9 166.2 %all-gather.5.cloned.1.call-start = ((), (), s32[]{:S(2)}) async-start(), calls=%async_computation.3 | async-start | bytes 5160960 | tf_op jit(solution)/shard_map/all_gather | solution.py:60
  10.0 6.1 %copy-start.8 = (s32[32,14]{0,1:T(8,128)S(1)}, s32[32,14]{0,1:T(8,128)}, u32[]{:S(2)}) copy-start(s32[32,14]{0,1:T(8,128)} %param.13) | copy-start | bytes 5380
  16.4 6.1 %copy-start.9 = (s32[32,14]{0,1:T(8,128)S(1)}, s32[32,14]{0,1:T(8,128)}, u32[]{:S(2)}) copy-start(s32[32,14]{0,1:T(8,128)} %param.12) | copy-start | bytes 5380
  28.8 4.4 %copy-start = (bf16[2048,896]{0,1:T(8,128)(2,1)S(1)}, bf16[2048,896]{0,1:T(8,128)(2,1)}, u32[]{:S(2)}) copy-start(bf16[2048,896]{0,1:T(8,128)(2,1)} %copy.23) | copy-start | bytes 11010052
  33.2 3.4 %copy-start.1 = (bf16[2048,896]{0,1:T(8,128)(2,1)S(1)}, bf16[2048,896]{0,1:T(8,128)(2,1)}, u32[]{:S(2)}) copy-start(bf16[2048,896]{0,1:T(8,128)(2,1)} %copy.22) | copy-start | bytes 11010052
  61.9 6.5 %copy-start.2 = (bf16[2048,896]{0,1:T(8,128)(2,1)S(1)}, bf16[2048,896]{0,1:T(8,128)(2,1)}, u32[]{:S(2)}) copy-start(bf16[2048,896]{0,1:T(8,128)(2,1)} %bitcast_multiply_fusion.1) | copy-start | bytes 11010052
  61.9 6.6 %copy-start.10 = (bf16[768,4096]{1,0:T(8,128)(2,1)S(1)}, bf16[768,4096]{1,0:T(8,128)(2,1)}, u32[]{:S(2)}) copy-start(bf16[768,4096]{1,0:T(8,128)(2,1)} %all-gather.3.cloned.1.call-done) | copy-start | bytes 18874372
  68.4 3.5 %copy-start.4 = (bf16[2048,896]{0,1:T(8,128)(2,1)S(1)}, bf16[2048,896]{0,1:T(8,128)(2,1)}, u32[]{:S(2)}) copy-start(bf16[2048,896]{0,1:T(8,128)(2,1)} %bitcast_multiply_fusion.2) | copy-start | bytes 11010052
  175.1 6.1 %copy-start.5 = (bf16[2048,896]{0,1:T(8,128)(2,1)S(1)}, bf16[2048,896]{0,1:T(8,128)(2,1)}, u32[]{:S(2)}) copy-start(bf16[2048,896]{0,1:T(8,128)(2,1)} %bitcast_multiply_fusion.2) | copy-start | bytes 11010052
  175.1 6.1 %copy-start.11 = (bf16[768,2688]{1,0:T(8,128)(2,1)S(1)}, bf16[768,2688]{1,0:T(8,128)(2,1)}, u32[]{:S(2)}) copy-start(bf16[768,2688]{1,0:T(8,128)(2,1)} %all-gather.5.cloned.1.call-done) | copy-start | bytes 12386308
  181.2 3.4 %copy-start.3 = (bf16[2048,896]{0,1:T(8,128)(2,1)S(1)}, bf16[2048,896]{0,1:T(8,128)(2,1)}, u32[]{:S(2)}) copy-start(bf16[2048,896]{0,1:T(8,128)(2,1)} %bitcast_multiply_fusion.1) | copy-start | bytes 11010052
  191.8 85.2 %all-to-all-start.1 = ((bf16[32,24,4096]{2,1,0:T(8,128)(2,1)}), bf16[32,24,4096]{2,1,0:T(8,128)(2,1)}, u32[]{:S(2)}, u32[]{:S(2)}) async-start(bf16[32,24,4096]{2,1,0:T(8,128)(2,1)} %bitcast.20), calls=%async_computation.1 | async-start | bytes 12582912 | tf_op jit(solution)/shard_map/all_to_all | solution.py:71
  218.2 14.7 %slice-start = ((s8[6291456]{0:T(1024)(128)(4,1)}), s8[2097152]{0:T(1024)(128)(4,1)S(1)}, s32[]{:S(2)}) async-start(s8[6291456]{0:T(1024)(128)(4,1)} %bitcast.25), calls=%async_computation.4 | async-start | bytes 4194304
  224.4 8.5 %copy-start.6 = (bf16[2048,896]{1,0:T(8,128)(2,1)S(1)}, bf16[2048,896]{1,0:T(8,128)(2,1)}, u32[]{:S(2)}) copy-start(bf16[2048,896]{1,0:T(8,128)(2,1)} %copy.27) | copy-start | bytes 11010052
  224.4 8.5 %slice-start.1 = ((s8[6291456]{0:T(1024)(128)(4,1)}), s8[4194304]{0:T(1024)(128)(4,1)S(1)}, s32[]{:S(2)}) async-start(s8[6291456]{0:T(1024)(128)(4,1)} %bitcast.25), calls=%async_computation.5 | async-start | bytes 8388608
  224.4 8.5 %copy-start.12 = (bf16[768,2688]{1,0:T(8,128)(2,1)S(1)}, bf16[768,2688]{1,0:T(8,128)(2,1)}, u32[]{:S(2)}) copy-start(bf16[768,2688]{1,0:T(8,128)(2,1)} %all-gather.5.cloned.1.call-done) | copy-start | bytes 12386308
  232.9 5.1 %copy-start.7 = (bf16[2048,896]{1,0:T(8,128)(2,1)S(1)}, bf16[2048,896]{1,0:T(8,128)(2,1)}, u32[]{:S(2)}) copy-start(bf16[2048,896]{1,0:T(8,128)(2,1)} %copy.26) | copy-start | bytes 11010052
Sparse Core Ops, SparseCore 0:
  10.2 51.5 all-gather.2
  130.5 44.5 all-gather.4
where the time goes:
time: 290 us; the launch traced here: 289 us
  waiting for transfers between devices  102 us (35%)
  blocking collectives  52.6 us (18%)
  local copies, waits for them, and re-layouts  46.2 us (16%)
  matrix products  45.3 us (16%)
  other arithmetic  20.9 us (7%)
  between operations  14.3 us (5%)
  starting transfers between devices  7.65 us (3%)
    all_to_all x1, blocking collectives, body(): swapped = lax.all_to_all(parts, 'row', 0, 0, tiled=True)  52.6 us
    all_gather x1, waiting for transfers between devices, body(): lax.all_gather(jnp.concatenate([hidden, dgate, dup], axis=1), 'row', axis...  44.7 us
    all_to_all x1, waiting for transfers between devices, body(): spread = lax.all_to_all(both, 'col', 0, 0, tiled=True)  33.9 us
    all_gather x1, waiting for transfers between devices, body(): lax.all_gather(jnp.concatenate([tokens, cotangent], axis=1), 'col', axis=...  23.2 us
    unnamed x33, local copies, waits for them, and re-layouts  19.5 us
    convert_element_type x7, local copies, waits for them, and re-layouts, expand(): return jnp.repeat(jnp.repeat(mask, BLOCK, 0), BLOCK, 1).astype(jnp.bfloat16)  18.9 us
    dot_general x3, matrix products, contract_first(): lax.dot_general(left, right, (((0,), (0,)), ((), ())), preferred_element_...  18.7 us
    dot_general x3, matrix products, contract_last(): lax.dot_general(left, right, (((1,), (1,)), ((), ())), preferred_element_...  13.7 us
  transfers between devices with their start and end apart: 3, of which 3 were waited for; matrix products, arithmetic and copies ran while one was open for 25% of the time, Pallas kernels for 0%

commit v1 on v0

--- a/solution.py
+++ b/solution.py
@@ -37,7 +37,10 @@
     w_up = up_weight * keep_up
     w_down = down_weight * keep_down
     width = w_gate.shape[1]
-    pair = lax.all_gather(jnp.concatenate([tokens, cotangent], axis=1), "col", axis=0, tiled=True)
+    x = jnp.concatenate([tokens, cotangent], axis=1)
+    size = lax.axis_size("col")
+    repeats = [size if d == 0 else 1 for d in range(x.ndim)]
+    pair = lax.all_to_all(jnp.tile(x, repeats), "col", split_axis=0, concat_axis=0, tiled=True)
     depth = tokens.shape[1]
     panel = pair[:, :depth]
     cot_panel = pair[:, depth:]

time: 290 us -> 329 us (1.13)
  waiting for transfers between devices: 102 us -> 126 us
  matrix products: 45.3 us -> 54.1 us
  starting transfers between devices: 7.65 us -> 15.9 us
  blocking collectives: 52.6 us -> 48.5 us
    all_to_all x0 -> x1, waiting for transfers between devices: none -> 48.8 us  [body(): lax.all_to_all(jnp.tile(x, repeats), 'col', split_axis=0, concat_axis=0,...]
    all_gather x1 -> x0, waiting for transfers between devices: 23.2 us -> none  [body(): lax.all_gather(jnp.concatenate([tokens, cotangent], axis=1), 'col', axis=...]
    all_to_all x0 -> x1, starting transfers between devices: none -> 8.52 us  [body(): lax.all_to_all(jnp.tile(x, repeats), 'col', split_axis=0, concat_axis=0,...]
    dot_general x3, matrix products: 18.7 us -> 23.4 us  [contract_first(): lax.dot_general(left, right, (((0,), (0,)), ((), ())), preferred_element_...]
    all_to_all x1, waiting for transfers between devices: 33.9 us -> 29.6 us  [body(): spread = lax.all_to_all(both, 'col', 0, 0, tiled=True)]
    all_to_all x1, blocking collectives: 52.6 us -> 48.5 us  [body(): swapped = lax.all_to_all(parts, 'row', 0, 0, tiled=True)]
    another operation x0 -> x1, local copies, waits for them, and re-layouts: none -> 3.41 us  [body(): jnp.tile(x, repeats)]
    unnamed x33 -> x29, local copies, waits for them, and re-layouts: 19.5 us -> 19.5 us
  transfers between devices with their start and end apart: 3 -> 3, of which waited for: 3 -> 3; matrix products, arithmetic and copies ran while one was open for 25% -> 23% of each run, Pallas kernels for 0% -> 0%
where the time goes in v1:
time: 329 us; the launch traced here: 327 us
  waiting for transfers between devices  126 us (38%)
  matrix products  54.1 us (16%)
  local copies, waits for them, and re-layouts  49.4 us (15%)
  blocking collectives  48.5 us (15%)
  other arithmetic  19.6 us (6%)
  starting transfers between devices  15.9 us (5%)
  between operations  14.3 us (4%)
    all_to_all x1, waiting for transfers between devices, body(): lax.all_to_all(jnp.tile(x, repeats), 'col', split_axis=0, concat_axis=0,...  48.8 us
    all_to_all x1, blocking collectives, body(): swapped = lax.all_to_all(parts, 'row', 0, 0, tiled=True)  48.5 us
    all_gather x1, waiting for transfers between devices, body(): lax.all_gather(jnp.concatenate([hidden, dgate, dup], axis=1), 'row', axis...  47.4 us
    all_to_all x1, waiting for transfers between devices, body(): spread = lax.all_to_all(both, 'col', 0, 0, tiled=True)  29.6 us
    dot_general x3, matrix products, contract_first(): lax.dot_general(left, right, (((0,), (0,)), ((), ())), preferred_element_...  23.4 us
    unnamed x29, local copies, waits for them, and re-layouts  19.5 us
    convert_element_type x7, local copies, waits for them, and re-layouts, expand(): return jnp.repeat(jnp.repeat(mask, BLOCK, 0), BLOCK, 1).astype(jnp.bfloat16)  18.8 us
    dot_general x3, matrix products, contract_last(): lax.dot_general(left, right, (((1,), (1,)), ((), ())), preferred_element_...  13.7 us
  transfers between devices with their start and end apart: 3, of which 3 were waited for; matrix products, arithmetic and copies ran while one was open for 23% of the time, Pallas kernels for 0%

profile of v1, /device:TPU:0, one launch (start us, length us, event | category | flops | bytes accessed | tf_op | source)
XLA Modules:
  0.0 327.5 jit_solution(9567393655685182213)
XLA Ops:
  7.2 1.0 pad_maximum_fusion.3
  8.1 3.4 %tile.2 = bf16[32,24,4096]{2,1,0:T(8,128)(2,1)} broadcast(bf16[24,4096]{1,0:T(8,128)(2,1)S(1)} %pad_maximum_fusion.3), dimensions={1,2} | broadcast | bytes 6488064 | tf_op jit(solution)/shard_map/tile | solution.py:43
  11.5 8.5 %all-to-all-start = ((bf16[32,24,4096]{2,1,0:T(8,128)(2,1)}), bf16[32,24,4096]{2,1,0:T(8,128)(2,1)}, u32[]{:S(2)}, u32[]{:S(2)}) async-start(bf16[32,24,4096]{2,1,0:T(8,128)(2,1)} %tile.2), calls=%async_computation | async-start | bytes 12582912 | tf_op jit(solution)/shard_map/all_to_all | solution.py:43
  20.1 0.0 all-gather.2.cloned.1.call-start
  20.1 0.1 copy.24
  20.2 0.1 broadcast_in_dim.22
  20.4 0.1 convert_element_type.89
  20.5 6.1 %copy.25 = bf16[896,2048]{0,1:T(8,128)(2,1)} copy(bf16[896,2048]{1,0:T(8,128)(2,1)} %param.11) | data formatting | bytes 7340032 | tf_op args[3]
  26.6 0.1 broadcast_in_dim.20
  26.7 0.1 convert_element_type.85
  26.9 0.0 copy-start.10
  26.9 6.1 %copy.23 = bf16[2048,896]{0,1:T(8,128)(2,1)} copy(bf16[2048,896]{1,0:T(8,128)(2,1)} %param.10) | data formatting | bytes 7340032 | tf_op args[2]
  33.0 0.1 broadcast_in_dim.18
  33.1 0.1 convert_element_type.81
  33.2 6.1 %copy.22 = bf16[2048,896]{0,1:T(8,128)(2,1)} copy(bf16[2048,896]{1,0:T(8,128)(2,1)} %param.9) | data formatting | bytes 7340032 | tf_op args[1]
  39.3 4.4 %bitcast_multiply_fusion = bf16[896,2048]{0,1:T(8,128)(2,1)} fusion(bf16[896,2048]{0,1:T(8,128)(2,1)} %copy.25, bf16[896,32]{0,1:T(8,128)(2,1)S(1)} %convert_element_type.89), kind=kLoop, calls=%fused_computation.17 | loop fusion | flops 1835008 | bytes 7397376 | tf_op jit(solution)/shard_map/mul | solution.py:38
  43.7 2.1 bitcast_multiply_fusion.1
  45.8 1.2 copy-done.1
  47.1 2.1 bitcast_multiply_fusion.2
  49.2 48.8 %all-to-all-done = bf16[32,24,4096]{2,1,0:T(8,128)(2,1)} async-done(((bf16[32,24,4096]{2,1,0:T(8,128)(2,1)}), bf16[32,24,4096]{2,1,0:T(8,128)(2,1)}, u32[]{:S(2)}, u32[]{:S(2)}) %all-to-all-start) | async-done | bytes 6291488 | tf_op jit(solution)/shard_map/all_to_all | solution.py:43
  98.0 6.5 %fusion.15 = bf16[768,896]{1,0:T(8,128)(2,1)S(1)} fusion(bf16[896,2048]{0,1:T(8,128)(2,1)} %bitcast_multiply_fusion, bf16[768,4096]{1,0:T(8,128)(2,1)} %bitcast), kind=kOutput, calls=%fused_computation.22 | convolution fusion | flops 2819260416 | bytes 8192000 | tf_op jit(solution)/shard_map/dot_general | solution.py:14
  104.5 0.0 copy-start.4
  104.5 5.6 %fusion.12 = bf16[768,896]{1,0:T(8,128)(2,1)S(1)} fusion(bf16[2048,896]{0,1:T(8,128)(2,1)S(1)} %copy-done.2, bf16[768,4096]{1,0:T(8,128)(2,1)} %bitcast), kind=kOutput, calls=%fused_computation.21 | convolution fusion | flops 2819260416 | bytes 8192000 | tf_op jit(solution)/shard_map/dot_general | solution.py:50
  110.1 5.4 %fusion.9 = bf16[768,896]{1,0:T(8,128)(2,1)S(1)} fusion(bf16[2048,896]{0,1:T(8,128)(2,1)S(1)} %copy-done.4, bf16[768,4096]{1,0:T(8,128)(2,1)} %bitcast), kind=kOutput, calls=%fused_computation.20 | convolution fusion | flops 2819260416 | bytes 8192000 | tf_op jit(solution)/shard_map/dot_general | solution.py:49
  115.6 0.4 pad_maximum_fusion.1
  115.9 48.5 %all_to_all.27 = bf16[4,192,2688]{2,1,0:T(8,128)(2,1)S(1)} all-to-all(bf16[4,192,2688]{2,1,0:T(8,128)(2,1)S(1)} %bitcast.22), channel_id=1, replica_groups=mesh['row'=4,'col'=32] {'row'}, dimensions={0} | all-to-all | bytes 8257536 | tf_op jit(solution)/shard_map/all_to_all | solution.py:56
  164.4 0.6 convert_reduce_fusion
  165.1 0.4 multiply_convert_fusion.5
  165.5 1.1 pad_maximum_fusion.2
  166.5 0.0 all-gather.2.cloned.1.call-update
  166.6 47.4 %all-gather.2.cloned.1.call-done = bf16[768,2688]{1,0:T(8,128)(2,1)} async-done(((bf16[192,2688]{1,0:T(8,128)(2,1)}), bf16[768,2688]{1,0:T(8,128)(2,1)}) %all-gather.2.cloned.1.call-update) | async-done | bytes 4128784 | tf_op jit(solution)/shard_map/all_gather | solution.py:63
  213.9 6.0 %convolution_convert_fusion = bf16[768,2048]{1,0:T(8,128)(2,1)S(1)} fusion(bf16[896,2048]{0,1:T(8,128)(2,1)} %bitcast_multiply_fusion, bf16[768,2688]{1,0:T(8,128)(2,1)} %all-gather.2.cloned.1.call-done), kind=kOutput, calls=%fused_computation.7 | convolution fusion | flops 2820145152 | bytes 8192000 | tf_op jit(solution)/shard_map/dot_general | solution.py:69
  220.0 3.4 %fusion.21 = f32[768,2048]{1,0:T(8,128)S(1)} fusion(bf16[2048,896]{0,1:T(8,128)(2,1)S(1)} %copy-done.5, bf16[768,2688]{1,0:T(8,128)(2,1)S(1)} %copy-done.11), kind=kOutput, calls=%fused_computation.26 | convolution fusion | flops 2818572288 | bytes 11337728 | tf_op jit(solution)/shard_map/dot_general | solution.py:14
  223.4 3.7 %add_convert_fusion = bf16[768,2048]{1,0:T(8,128)(2,1)S(1)} fusion(f32[768,2048]{1,0:T(8,128)S(1)} %fusion.21, bf16[2048,896]{0,1:T(8,128)(2,1)S(1)} %copy-done.3, bf16[768,2688]{1,0:T(8,128)(2,1)S(1)} %copy-done.11), kind=kOutput, calls=%fused_computation.5 | convolution fusion | flops 2821718016 | bytes 14483456 | tf_op jit(solution)/shard_map/dot_general | solution.py:14
  227.2 3.4 %pad_maximum_fusion = bf16[768,4096]{1,0:T(8,128)(2,1)} fusion(bf16[768,2048]{1,0:T(8,128)(2,1)S(1)} %add_convert_fusion, bf16[768,2048]{1,0:T(8,128)(2,1)S(1)} %convolution_convert_fusion), kind=kLoop, calls=%fused_computation.4 | loop fusion | flops 12582912 | bytes 12582912 | tf_op jit(solution)/shard_map/concatenate | solution.py:67
  230.6 7.3 %all-to-all-start.2 = ((bf16[32,24,4096]{2,1,0:T(8,128)(2,1)}), bf16[32,24,4096]{2,1,0:T(8,128)(2,1)}, u32[]{:S(2)}, u32[]{:S(2)}) async-start(bf16[32,24,4096]{2,1,0:T(8,128)(2,1)} %bitcast.21), calls=%async_computation.2 | async-start | bytes 12582912 | tf_op jit(solution)/shard_map/all_to_all | solution.py:74
  237.9 2.1 broadcast_in_dim.23
  240.1 6.1 %copy.28 = bf16[896,2048]{1,0:T(8,128)(2,1)} copy(bf16[896,2048]{0,1:T(8,128)(2,1)} %bitcast.23) | data formatting | bytes 7340032 | tf_op jit(solution)/shard_map/convert_element_type | solution.py:10
  246.2 2.3 broadcast_in_dim.21
  248.5 6.0 %copy.27 = bf16[2048,896]{1,0:T(8,128)(2,1)} copy(bf16[2048,896]{0,1:T(8,128)(2,1)} %bitcast.24) | data formatting | bytes 7340032 | tf_op jit(solution)/shard_map/convert_element_type | solution.py:10
  254.5 2.3 broadcast_in_dim.19
  256.8 6.0 %copy.26 = bf16[2048,896]{1,0:T(8,128)(2,1)} copy(bf16[2048,896]{0,1:T(8,128)(2,1)} %bitcast.25) | data formatting | bytes 7340032 | tf_op jit(solution)/shard_map/convert_element_type | solution.py:10
  262.9 8.5 %multiply_convert_fusion = bf16[896,2048]{1,0:T(8,128)(2,1)} fusion(bf16[896,2048]{1,0:T(8,128)(2,1)} %copy.28, bf16[768,4096]{1,0:T(8,128)(2,1)} %bitcast, bf16[768,2688]{1,0:T(8,128)(2,1)} %all-gather.2.cloned.1.call-done), kind=kOutput, calls=%fused_computation.1 | convolution fusion | flops 2824077312 | bytes 11862016 | tf_op jit(solution)/shard_map/dot_general | solution.py:20
  271.4 7.5 %multiply_convert_fusion.1 = bf16[2048,896]{1,0:T(8,128)(2,1)} fusion(bf16[2048,896]{1,0:T(8,128)(2,1)S(1)} %copy-done.6, bf16[768,4096]{1,0:T(8,128)(2,1)} %bitcast, bf16[768,2688]{1,0:T(8,128)(2,1)S(1)} %copy-done.12), kind=kOutput, calls=%fused_computation.2 | convolution fusion | flops 2824077312 | bytes 11862016 | tf_op jit(solution)/shard_map/dot_general | solution.py:20
  278.9 7.4 %multiply_convert_fusion.2 = bf16[2048,896]{1,0:T(8,128)(2,1)} fusion(bf16[2048,896]{1,0:T(8,128)(2,1)S(1)} %copy-done.7, bf16[768,4096]{1,0:T(8,128)(2,1)} %bitcast, bf16[768,2688]{1,0:T(8,128)(2,1)S(1)} %copy-done.12), kind=kOutput, calls=%fused_computation.3 | convolution fusion | flops 2824077312 | bytes 11862016 | tf_op jit(solution)/shard_map/dot_general | solution.py:20
  286.3 29.6 %all-to-all-done.2 = bf16[32,24,4096]{2,1,0:T(8,128)(2,1)} async-done(((bf16[32,24,4096]{2,1,0:T(8,128)(2,1)}), bf16[32,24,4096]{2,1,0:T(8,128)(2,1)}, u32[]{:S(2)}, u32[]{:S(2)}) %all-to-all-start.2) | async-done | bytes 6291488 | tf_op jit(solution)/shard_map/all_to_all | solution.py:74
  315.8 4.1 %reduce_sum.22 = bf16[24,4096]{1,0:T(8,128)(2,1)S(1)} reduce(bf16[32,24,4096]{2,1,0:T(8,128)(2,1)} %all-to-all-done.2, bf16[]{:T(256)} %constant.7.clone.1), dimensions={0}, to_apply=%region_1.2 | reduce | flops 3047424 | bytes 6488066 | tf_op jit(solution)/shard_map/reduce_sum | solution.py:79
  319.9 0.7 fusion.25
  (26 shorter events, 0.1 us)
Async XLA Ops:
  11.5 8.6 %copy-start.8 = (s32[14,32]{1,0:T(8,128)S(1)}, s32[14,32]{1,0:T(8,128)}, u32[]{:S(2)}) copy-start(s32[14,32]{1,0:T(8,128)} %param.14) | copy-start | bytes 5380
  11.5 86.4 %all-to-all-start = ((bf16[32,24,4096]{2,1,0:T(8,128)(2,1)}), bf16[32,24,4096]{2,1,0:T(8,128)(2,1)}, u32[]{:S(2)}, u32[]{:S(2)}) async-start(bf16[32,24,4096]{2,1,0:T(8,128)(2,1)} %tile.2), calls=%async_computation | async-start | bytes 12582912 | tf_op jit(solution)/shard_map/all_to_all | solution.py:43
  20.1 193.9 %all-gather.2.cloned.1.call-start = ((), (), s32[]{:S(2)}) async-start(), calls=%async_computation.3 | async-start | bytes 5160960 | tf_op jit(solution)/shard_map/all_gather | solution.py:63
  20.5 6.1 %copy-start.9 = (s32[32,14]{0,1:T(8,128)S(1)}, s32[32,14]{0,1:T(8,128)}, u32[]{:S(2)}) copy-start(s32[32,14]{0,1:T(8,128)} %param.13) | copy-start | bytes 5380
  26.9 6.1 %copy-start.10 = (s32[32,14]{0,1:T(8,128)S(1)}, s32[32,14]{0,1:T(8,128)}, u32[]{:S(2)}) copy-start(s32[32,14]{0,1:T(8,128)} %param.12) | copy-start | bytes 5380
  39.3 4.4 %copy-start = (bf16[2048,896]{0,1:T(8,128)(2,1)S(1)}, bf16[2048,896]{0,1:T(8,128)(2,1)}, u32[]{:S(2)}) copy-start(bf16[2048,896]{0,1:T(8,128)(2,1)} %copy.23) | copy-start | bytes 11010052
  43.7 3.4 %copy-start.1 = (bf16[2048,896]{0,1:T(8,128)(2,1)S(1)}, bf16[2048,896]{0,1:T(8,128)(2,1)}, u32[]{:S(2)}) copy-start(bf16[2048,896]{0,1:T(8,128)(2,1)} %copy.22) | copy-start | bytes 11010052
  98.0 6.5 %copy-start.2 = (bf16[2048,896]{0,1:T(8,128)(2,1)S(1)}, bf16[2048,896]{0,1:T(8,128)(2,1)}, u32[]{:S(2)}) copy-start(bf16[2048,896]{0,1:T(8,128)(2,1)} %bitcast_multiply_fusion.1) | copy-start | bytes 11010052
  104.5 5.6 %copy-start.4 = (bf16[2048,896]{0,1:T(8,128)(2,1)S(1)}, bf16[2048,896]{0,1:T(8,128)(2,1)}, u32[]{:S(2)}) copy-start(bf16[2048,896]{0,1:T(8,128)(2,1)} %bitcast_multiply_fusion.2) | copy-start | bytes 11010052
  213.9 6.1 %copy-start.5 = (bf16[2048,896]{0,1:T(8,128)(2,1)S(1)}, bf16[2048,896]{0,1:T(8,128)(2,1)}, u32[]{:S(2)}) copy-start(bf16[2048,896]{0,1:T(8,128)(2,1)} %bitcast_multiply_fusion.2) | copy-start | bytes 11010052
  213.9 6.1 %copy-start.11 = (bf16[768,2688]{1,0:T(8,128)(2,1)S(1)}, bf16[768,2688]{1,0:T(8,128)(2,1)}, u32[]{:S(2)}) copy-start(bf16[768,2688]{1,0:T(8,128)(2,1)} %all-gather.2.cloned.1.call-done) | copy-start | bytes 12386308
  220.0 3.4 %copy-start.3 = (bf16[2048,896]{0,1:T(8,128)(2,1)S(1)}, bf16[2048,896]{0,1:T(8,128)(2,1)}, u32[]{:S(2)}) copy-start(bf16[2048,896]{0,1:T(8,128)(2,1)} %bitcast_multiply_fusion.1) | copy-start | bytes 11010052
  230.6 85.2 %all-to-all-start.2 = ((bf16[32,24,4096]{2,1,0:T(8,128)(2,1)}), bf16[32,24,4096]{2,1,0:T(8,128)(2,1)}, u32[]{:S(2)}, u32[]{:S(2)}) async-start(bf16[32,24,4096]{2,1,0:T(8,128)(2,1)} %bitcast.21), calls=%async_computation.2 | async-start | bytes 12582912 | tf_op jit(solution)/shard_map/all_to_all | solution.py:74
  262.9 8.5 %copy-start.6 = (bf16[2048,896]{1,0:T(8,128)(2,1)S(1)}, bf16[2048,896]{1,0:T(8,128)(2,1)}, u32[]{:S(2)}) copy-start(bf16[2048,896]{1,0:T(8,128)(2,1)} %copy.27) | copy-start | bytes 11010052
  262.9 8.5 %copy-start.12 = (bf16[768,2688]{1,0:T(8,128)(2,1)S(1)}, bf16[768,2688]{1,0:T(8,128)(2,1)}, u32[]{:S(2)}) copy-start(bf16[768,2688]{1,0:T(8,128)(2,1)} %all-gather.2.cloned.1.call-done) | copy-start | bytes 12386308
  271.3 7.5 %copy-start.7 = (bf16[2048,896]{1,0:T(8,128)(2,1)S(1)}, bf16[2048,896]{1,0:T(8,128)(2,1)}, u32[]{:S(2)}) copy-start(bf16[2048,896]{1,0:T(8,128)(2,1)} %copy.26) | copy-start | bytes 11010052
Sparse Core Ops, SparseCore 0:
  166.7 47.1 all-gather.1
